TPU v7x, 512 devices: a whole 4x8x8 slice. The times are simulated.
512 devices in a mesh: dp: 16 (over z, core), seq: 32 (over x, y).
Axes of the slice: x: 4, y: 8, z: 8, core: 2. Of those that a mesh axis runs over, the one named last changes fastest.
Arguments:
- inputs: bfloat16 [16, 4096, 4096], P('dp', 'seq'), may hold values from -6 to 6
- out_grads: bfloat16 [16, 4096, 14336], P('dp', 'seq'), may hold values from -6 to 6
- valid: int32 [16, 4096], P('dp', 'seq'), may hold values 0 or 1
- doc_blocks: int32 [16, 4], P('dp'), may hold values from 1 to 16, 32 in all within a row
- doc_ids: int32 [64], replicated, may hold values from 0 to 63, each once
- proj_in: bfloat16 [4096, 64], P('seq'), may hold values from -0.09375 to 0.09375
- proj_out: bfloat16 [14336, 64], P('seq'), may hold values from -0.046875 to 0.046875
- test_grads: bfloat16 [1024, 4096], P('seq'), may hold values from -192 to 192
Outputs:
- scores: float32 [64, 1024], P(None, 'seq')
Inputs may be any that keep to these rules, and one draw needn't show every extreme that they name: `doc_blocks`: each group's lengths sum to 32; the largest is 16 in every group. `doc_ids`: every document number appears once.
All inputs are finite; a program needn't handle non-finite values. No bound on the sum of `valid` on one device may be relied on, other than what follows from the above.
Results may differ from a plain program's by a relative error of at most 0.0003.
Values may be sent and summed in bfloat16 or wider, within the bound.
A program may use at most 64 MiB of HBM per device.

v0:
```python
import jax
import jax.numpy as jnp
from jax import lax
from jax.sharding import PartitionSpec as P

PROJ_OUT = 64
FEAT = 4096
BLOCK = 128
DOC_GRP = 4


def per_device(inputs, out_grads, valid, doc_blocks, doc_ids, proj_in, proj_out, test_grads):
    tokens = inputs[0]
    outgrad = out_grads[0]
    slots = tokens.shape[0]
    columns = tokens
    px = jnp.dot(
        columns,
        lax.all_gather(proj_in, "seq", axis=0, tiled=True),
        preferred_element_type=jnp.float32,
    )
    columns = outgrad
    pg = jnp.dot(
        columns,
        lax.all_gather(proj_out, "seq", axis=0, tiled=True),
        preferred_element_type=jnp.float32,
    )
    ends = jnp.cumsum(doc_blocks[0])
    position = lax.axis_index("seq") * slots + jnp.arange(slots, dtype=jnp.int32)
    blk = position // BLOCK
    owner = jnp.sum((blk[:, None] >= ends[None, :]).astype(jnp.int32), axis=1)
    onehot = (
        (owner[:, None] == jnp.arange(DOC_GRP, dtype=jnp.int32)[None, :]) & (valid[0][:, None] == 1)
    ).astype(jnp.float32)
    weighted = (onehot[:, :, None] * pg[:, None, :]).reshape(slots, DOC_GRP * PROJ_OUT)
    partial_grads = jnp.dot(weighted.T, px, precision=lax.Precision.HIGHEST).reshape(DOC_GRP, FEAT)
    ndocs = DOC_GRP * lax.axis_size("dp")
    group_grads = lax.psum(partial_grads, "seq")
    doc_grads = lax.all_gather(group_grads, "dp", axis=0, tiled=True)
    gram = jnp.dot(doc_grads, doc_grads.T, precision=lax.Precision.HIGHEST)
    cross = jnp.dot(doc_grads, test_grads.astype(jnp.float32).T, precision=lax.Precision.HIGHEST)
    damp = 0.1 * jnp.trace(gram) / ndocs
    matrix = gram / ndocs + damp * jnp.eye(ndocs, dtype=jnp.float32)
    factor = jnp.linalg.cholesky(matrix)
    middle = lax.linalg.triangular_solve(factor, cross, left_side=True, lower=True)
    solved = lax.linalg.triangular_solve(
        factor, middle, left_side=True, lower=True, transpose_a=True
    )
    placing = (doc_ids[None, :] == jnp.arange(ndocs, dtype=jnp.int32)[:, None]).astype(jnp.float32)
    return jnp.dot(placing, solved, precision=lax.Precision.HIGHEST)


def solution(mesh):
    in_specs = (
        P("dp", "seq", None),
        P("dp", "seq", None),
        P("dp", "seq"),
        P("dp", None),
        P(),
        P("seq", None),
        P("seq", None),
        P("seq", None),
    )
    out_specs = P(None, "seq")
    return jax.shard_map(
        per_device, mesh=mesh, in_specs=in_specs, out_specs=out_specs, check_vma=False
    )
```

profile of v0, /device:TPU:1, one launch (start us, length us, event | category | flops | bytes accessed | tf_op | source)
XLA Modules:
  0.0 325.9 jit_solution(14330074124522014039)
XLA Ops:
  6.5 0.7 all-gather.5.cloned.1.call-update
  7.3 0.8 reduce-window.8
  8.1 0.1 convert_reduce_fusion
  8.2 41.4 %all_gather.10 = bf16[4096,64]{0,1:T(8,128)(2,1)S(1)} all-gather(bf16[128,64]{0,1:T(8,128)(2,1)} %param.13), channel_id=1, replica_groups=mesh['dp'=16,'seq'=32] {'seq'}, dimensions={0}, use_global_device_ids=true | all-gather | bytes 540672 | tf_op jit(solution)/shard_map/all_gather | solution.py:19
  49.6 0.7 compare_bitcast_fusion
  50.3 0.5 fusion.2
  50.8 44.7 %all-gather.5.cloned.1.call-done = bf16[32,448,64]{1,2,0:T(8,128)(2,1)} async-done(((bf16[1,448,64]{1,2,0:T(8,128)(2,1)}), bf16[32,448,64]{1,2,0:T(8,128)(2,1)}) %all-gather.5.cloned.1.call-update) | async-done | bytes 1835024 | tf_op jit(solution)/shard_map/all_gather | solution.py:25
  95.6 2.8 copy.20
  98.3 3.4 %reshape.113 = bf16[14336,64]{0,1:T(8,128)(2,1)} reshape(bf16[32,448,64]{1,0,2:T(8,128)(2,1)S(1)} %copy.20) | data formatting | bytes 3670016
  101.7 4.0 %fusion = f32[128,64]{0,1:T(8,128)S(1)} fusion(bf16[14336,64]{0,1:T(8,128)(2,1)} %reshape.113, bf16[1,128,14336]{2,1,0:T(8,128)(2,1)} %param.9), kind=kOutput, calls=%fused_computation | convolution fusion | flops 234881024 | bytes 5537792 | tf_op jit(solution)/shard_map/dot_general | solution.py:23
  105.7 0.3 fusion.15
  106.0 0.7 reshape.111
  106.8 147.6 %all-reduce.2.cloned.1.call-done = f32[4,4096]{1,0:T(4,128)} async-done(((f32[4,4096]{1,0:T(4,128)}), f32[4,4096]{1,0:T(4,128)}) %all-reduce.2.cloned.1.call-update) | async-done | bytes 65552 | tf_op jit(solution)/shard_map/psum | solution.py:38
  254.4 47.1 %all-gather.7.cloned.1.call-done = f32[16,4,4096]{2,1,0:T(4,128)} async-done(((f32[1,4,4096]{2,1,0:T(4,128)}), f32[16,4,4096]{2,1,0:T(4,128)}) %all-gather.7.cloned.1.call-update) | async-done | bytes 1048592 | tf_op jit(solution)/shard_map/all_gather | solution.py:39
  301.5 1.6 reshape.115
  303.1 1.6 select_reduce_fusion.1
  305.6 5.8 %cholesky.17 = f32[64,64]{1,0:T(8,128)S(1)} custom-call(f32[64,64]{1,0:T(8,128)S(1)} %fusion.10), custom_call_target="Cholesky" | custom-call | tf_op jit(solution)/shard_map/jit(cholesky)/cholesky | solution.py:44
  311.4 0.6 compare_reduce_fusion
  312.1 0.7 fusion.4
  312.8 4.9 %custom-call.8 = f32[1,64,64]{1,2,0:T(8,128)S(1)} custom-call(f32[1,64,64]{2,1,0:T(8,128)S(1)} %fusion.4), custom_call_target="InvertDiagBlocksLowerTriangular" | custom-call | tf_op jit(solution)/shard_map/triangular_solve | solution.py:46
  317.7 0.6 fusion.16
  318.3 0.1 fusion.7
  318.4 0.2 fusion.5
  318.6 0.8 fusion.11
  (19 shorter events, 0.4 us)
Async XLA Ops:
  6.5 43.8 %copy-start = (bf16[1,128,4096]{2,1,0:T(8,128)(2,1)S(1)}, bf16[1,128,4096]{2,1,0:T(8,128)(2,1)}, u32[]{:S(2)}) copy-start(bf16[1,128,4096]{2,1,0:T(8,128)(2,1)} %param.8) | copy-start | bytes 3145732
  6.5 89.0 %all-gather.5.cloned.1.call-start = ((), (), s32[]{:S(2)}) async-start(), calls=%async_computation.1 | async-start | bytes 2162688 | tf_op jit(solution)/shard_map/all_gather | solution.py:25
  7.3 247.2 %all-reduce.2.cloned.1.call-start = ((), (), s32[]{:S(2)}) async-start(), calls=%async_computation | async-start | bytes 131072 | tf_op jit(solution)/shard_map/psum | solution.py:38
  106.7 194.8 %all-gather.7.cloned.1.call-start = ((), (), s32[]{:S(2)}) async-start(), calls=%async_computation.2 | async-start | bytes 1114112 | tf_op jit(solution)/shard_map/all_gather | solution.py:39
  254.4 63.2 %copy-start.1 = (bf16[32,4096]{1,0:T(8,128)(2,1)S(1)}, bf16[32,4096]{1,0:T(8,128)(2,1)}, u32[]{:S(2)}) copy-start(bf16[32,4096]{1,0:T(8,128)(2,1)} %param.15) | copy-start | bytes 786436
  303.1 15.5 %copy-start.2 = (s32[64]{0:T(128)S(1)}, s32[64]{0:T(128)}, u32[]{:S(2)}) copy-start(s32[64]{0:T(128)} %param.12) | copy-start | bytes 772
Sparse Core Ops, SparseCore 0:
  10.5 84.9 all-gather.4
  106.8 147.5 all-reduce.1
  256.5 44.9 all-gather.6
where the time goes:
time: 326 us
  waiting for transfers between devices  240 us (74%)
  blocking collectives  41.4 us (13%)
  between operations  13.9 us (4%)
  other arithmetic  13.7 us (4%)
  local copies, waits for them, and re-layouts  8.61 us (3%)
  matrix products  8 us (2%)
    psum x1, waiting for transfers between devices, per_device(): group_grads = lax.psum(partial_grads, 'seq')  148 us
    all_gather x1, waiting for transfers between devices, per_device(): doc_grads = lax.all_gather(group_grads, 'dp', axis=0, tiled=True)  47.1 us
    all_gather x1, waiting for transfers between devices, per_device(): lax.all_gather(proj_out, 'seq', axis=0, tiled=True)  44.7 us
    all_gather x1, blocking collectives, per_device(): lax.all_gather(proj_in, 'seq', axis=0, tiled=True)  41.4 us
  transfers between devices with their start and end apart: 3, of which 3 were waited for; matrix products, arithmetic and copies ran while one was open for 1% of the time, Pallas kernels for 0%

commit v1 on v0

--- a/solution.py
+++ b/solution.py
@@ -35,7 +35,11 @@
     weighted = (onehot[:, :, None] * pg[:, None, :]).reshape(slots, DOC_GRP * PROJ_OUT)
     partial_grads = jnp.dot(weighted.T, px, precision=lax.Precision.HIGHEST).reshape(DOC_GRP, FEAT)
     ndocs = DOC_GRP * lax.axis_size("dp")
-    group_grads = lax.psum(partial_grads, "seq")
+    group_grads = partial_grads
+    for hop in (1, 2, 4, 8, 16):
+        group_grads = group_grads + lax.ppermute(
+            group_grads, "seq", [(dev, dev ^ hop) for dev in range(32)]
+        )
     doc_grads = lax.all_gather(group_grads, "dp", axis=0, tiled=True)
     gram = jnp.dot(doc_grads, doc_grads.T, precision=lax.Precision.HIGHEST)
     cross = jnp.dot(doc_grads, test_grads.astype(jnp.float32).T, precision=lax.Precision.HIGHEST)

time: 326 us -> 215 us (0.66)
  waiting for transfers between devices: 240 us -> 115 us
  starting transfers between devices: 0.08 us -> 13.6 us
    psum x1 -> x0, waiting for transfers between devices: 148 us -> none  [per_device(): group_grads = lax.psum(partial_grads, 'seq')]
    ppermute x0 -> x5, waiting for transfers between devices: none -> 18.4 us  [per_device(): lax.ppermute(group_grads, 'seq', [(dev, dev ^ hop) for dev in range(32)])]
    ppermute x0 -> x5, starting transfers between devices: none -> 13.5 us  [per_device(): lax.ppermute(group_grads, 'seq', [(dev, dev ^ hop) for dev in range(32)])]
    all_gather x1, waiting for transfers between devices: 47.1 us -> 50.7 us  [per_device(): doc_grads = lax.all_gather(group_grads, 'dp', axis=0, tiled=True)]
  transfers between devices with their start and end apart: 3 -> 7, of which waited for: 3 -> 7; matrix products, arithmetic and copies ran while one was open for 1% -> 1% of each run, Pallas kernels for 0% -> 0%
where the time goes in v1:
time: 215 us; the launch traced here: 214 us
  waiting for transfers between devices  115 us (53%)
  blocking collectives  41.4 us (19%)
  other arithmetic  14.4 us (7%)
  between operations  14.3 us (7%)
  starting transfers between devices  13.6 us (6%)
  matrix products  8.01 us (4%)
  local copies, waits for them, and re-layouts  8 us (4%)
    all_gather x1, waiting for transfers between devices, per_device(): doc_grads = lax.all_gather(group_grads, 'dp', axis=0, tiled=True)  50.7 us
    all_gather x1, waiting for transfers between devices, per_device(): lax.all_gather(proj_out, 'seq', axis=0, tiled=True)  44.7 us
    all_gather x1, blocking collectives, per_device(): lax.all_gather(proj_in, 'seq', axis=0, tiled=True)  41.4 us
    ppermute x5, waiting for transfers between devices, per_device(): lax.ppermute(group_grads, 'seq', [(dev, dev ^ hop) for dev in range(32)])  18.4 us
    ppermute x5, starting transfers between devices, per_device(): lax.ppermute(group_grads, 'seq', [(dev, dev ^ hop) for dev in range(32)])  13.5 us
    another operation x3, other arithmetic, per_device(): factor = jnp.linalg.cholesky(matrix)  6.52 us
    another operation x2, other arithmetic, per_device(): lax.linalg.triangular_solve(factor, middle, left_side=True, lower=True, t...  5.55 us
    unnamed x8, local copies, waits for them, and re-layouts  4.99 us
  transfers between devices with their start and end apart: 7, of which 7 were waited for; matrix products, arithmetic and copies ran while one was open for 1% of the time, Pallas kernels for 0%

profile of v1, /device:TPU:1, one launch (start us, length us, event | category | flops | bytes accessed | tf_op | source)
XLA Modules:
  0.0 214.1 jit_solution(16331824302549956291)
XLA Ops:
  6.5 0.7 all-gather.5.cloned.1.call-update
  7.3 0.8 reduce-window.8
  8.2 41.4 %all_gather.10 = bf16[4096,64]{0,1:T(8,128)(2,1)S(1)} all-gather(bf16[128,64]{0,1:T(8,128)(2,1)} %param.13), channel_id=1, replica_groups=mesh['dp'=16,'seq'=32] {'seq'}, dimensions={0}, use_global_device_ids=true | all-gather | bytes 540672 | tf_op jit(solution)/shard_map/all_gather | solution.py:19
  49.6 0.7 compare_bitcast_fusion
  50.8 44.7 %all-gather.5.cloned.1.call-done = bf16[32,448,64]{1,2,0:T(8,128)(2,1)} async-done(((bf16[1,448,64]{1,2,0:T(8,128)(2,1)}), bf16[32,448,64]{1,2,0:T(8,128)(2,1)}) %all-gather.5.cloned.1.call-update) | async-done | bytes 1835024 | tf_op jit(solution)/shard_map/all_gather | solution.py:25
  95.6 2.8 %copy.20 = bf16[32,448,64]{1,0,2:T(8,128)(2,1)S(1)} copy(bf16[32,448,64]{1,2,0:T(8,128)(2,1)} %all-gather.5.cloned.1.call-done) | data formatting | bytes 3670016 | tf_op jit(solution)/shard_map/all_gather | solution.py:25
  98.3 3.4 %reshape.113 = bf16[14336,64]{0,1:T(8,128)(2,1)} reshape(bf16[32,448,64]{1,0,2:T(8,128)(2,1)S(1)} %copy.20) | data formatting | bytes 3670016
  101.7 4.0 %fusion = f32[128,64]{0,1:T(8,128)S(1)} fusion(bf16[14336,64]{0,1:T(8,128)(2,1)} %reshape.113, bf16[1,128,14336]{2,1,0:T(8,128)(2,1)} %param.9), kind=kOutput, calls=%fused_computation | convolution fusion | flops 234881024 | bytes 5537792 | tf_op jit(solution)/shard_map/dot_general | solution.py:23
  106.1 2.0 collective-permute-start
  108.1 3.0 %collective-permute-done = f32[4,4096]{1,0:T(4,128)S(1)} collective-permute-done((f32[4,4096]{1,0:T(4,128)S(1)}, f32[4,4096]{1,0:T(4,128)S(1)}, u32[]{:S(2)}, u32[]{:S(2)}) %collective-permute-start) | collective-permute-done | bytes 65568 | tf_op jit(solution)/shard_map/ppermute | solution.py:40
  111.1 2.9 %collective-permute-start.1 = (f32[4,4096]{1,0:T(4,128)S(1)}, f32[4,4096]{1,0:T(4,128)S(1)}, u32[]{:S(2)}, u32[]{:S(2)}) collective-permute-start(f32[4,4096]{1,0:T(4,128)S(1)} %add.51), channel_id=1, source_target_pairs={{0,2},{1,3},{2,0},{3,1},{4,6},{5,7},{6,4},{7,5},{8,10},{9,11},{10,... | collective-permute-start | bytes 196616 | tf_op jit(solution)/shard_map/ppermute | solution.py:40
  114.0 3.5 %collective-permute-done.1 = f32[4,4096]{1,0:T(4,128)S(1)} collective-permute-done((f32[4,4096]{1,0:T(4,128)S(1)}, f32[4,4096]{1,0:T(4,128)S(1)}, u32[]{:S(2)}, u32[]{:S(2)}) %collective-permute-start.1) | collective-permute-done | bytes 65568 | tf_op jit(solution)/shard_map/ppermute | solution.py:40
  117.6 3.4 %collective-permute-start.2 = (f32[4,4096]{1,0:T(4,128)S(1)}, f32[4,4096]{1,0:T(4,128)S(1)}, u32[]{:S(2)}, u32[]{:S(2)}) collective-permute-start(f32[4,4096]{1,0:T(4,128)S(1)} %add.52), channel_id=1, source_target_pairs={{0,4},{1,5},{2,6},{3,7},{4,0},{5,1},{6,2},{7,3},{8,12},{9,13},{10,... | collective-permute-start | bytes 196616 | tf_op jit(solution)/shard_map/ppermute | solution.py:40
  121.0 5.5 %collective-permute-done.2 = f32[4,4096]{1,0:T(4,128)S(1)} collective-permute-done((f32[4,4096]{1,0:T(4,128)S(1)}, f32[4,4096]{1,0:T(4,128)S(1)}, u32[]{:S(2)}, u32[]{:S(2)}) %collective-permute-start.2) | collective-permute-done | bytes 65568 | tf_op jit(solution)/shard_map/ppermute | solution.py:40
  126.5 1.9 collective-permute-start.3
  128.5 3.1 %collective-permute-done.3 = f32[4,4096]{1,0:T(4,128)S(1)} collective-permute-done((f32[4,4096]{1,0:T(4,128)S(1)}, f32[4,4096]{1,0:T(4,128)S(1)}, u32[]{:S(2)}, u32[]{:S(2)}) %collective-permute-start.3) | collective-permute-done | bytes 65568 | tf_op jit(solution)/shard_map/ppermute | solution.py:40
  131.6 3.2 %collective-permute-start.4 = (f32[4,4096]{1,0:T(4,128)S(1)}, f32[4,4096]{1,0:T(4,128)S(1)}, u32[]{:S(2)}, u32[]{:S(2)}) collective-permute-start(f32[4,4096]{1,0:T(4,128)S(1)} %add.54), channel_id=1, source_target_pairs={{0,16},{1,17},{2,18},{3,19},{4,20},{5,21},{6,22},{7,23},{8,24},{9,... | collective-permute-start | bytes 196616 | tf_op jit(solution)/shard_map/ppermute | solution.py:40
  134.8 3.3 %collective-permute-done.4 = f32[4,4096]{1,0:T(4,128)S(1)} collective-permute-done((f32[4,4096]{1,0:T(4,128)S(1)}, f32[4,4096]{1,0:T(4,128)S(1)}, u32[]{:S(2)}, u32[]{:S(2)}) %collective-permute-start.4) | collective-permute-done | bytes 65568 | tf_op jit(solution)/shard_map/ppermute | solution.py:40
  138.8 50.7 %all-gather.7.cloned.1.call-done = f32[16,4,4096]{2,1,0:T(4,128)} async-done(((f32[1,4,4096]{2,1,0:T(4,128)}), f32[16,4,4096]{2,1,0:T(4,128)}) %all-gather.7.cloned.1.call-update) | async-done | bytes 1048592 | tf_op jit(solution)/shard_map/all_gather | solution.py:43
  189.5 1.6 reshape.115
  191.1 1.6 select_reduce_fusion.1
  193.5 5.8 %cholesky.17 = f32[64,64]{1,0:T(8,128)S(1)} custom-call(f32[64,64]{1,0:T(8,128)S(1)} %fusion.10), custom_call_target="Cholesky" | custom-call | tf_op jit(solution)/shard_map/jit(cholesky)/cholesky | solution.py:48
  200.7 4.9 %custom-call.8 = f32[1,64,64]{1,2,0:T(8,128)S(1)} custom-call(f32[1,64,64]{2,1,0:T(8,128)S(1)} %fusion.4), custom_call_target="InvertDiagBlocksLowerTriangular" | custom-call | tf_op jit(solution)/shard_map/triangular_solve | solution.py:50
  206.5 0.8 fusion.11
  (31 shorter events, 4.2 us)
Async XLA Ops:
  6.5 43.8 %copy-start = (bf16[1,128,4096]{2,1,0:T(8,128)(2,1)S(1)}, bf16[1,128,4096]{2,1,0:T(8,128)(2,1)}, u32[]{:S(2)}) copy-start(bf16[1,128,4096]{2,1,0:T(8,128)(2,1)} %param.8) | copy-start | bytes 3145732
  6.5 89.0 %all-gather.5.cloned.1.call-start = ((), (), s32[]{:S(2)}) async-start(), calls=%async_computation | async-start | bytes 2162688 | tf_op jit(solution)/shard_map/all_gather | solution.py:25
  7.3 182.2 %all-gather.7.cloned.1.call-start = ((), (), s32[]{:S(2)}) async-start(), calls=%async_computation.1 | async-start | bytes 1114112 | tf_op jit(solution)/shard_map/all_gather | solution.py:43
  106.1 5.0 %collective-permute-start = (f32[4,4096]{1,0:T(4,128)S(1)}, f32[4,4096]{1,0:T(4,128)S(1)}, u32[]{:S(2)}, u32[]{:S(2)}) collective-permute-start(f32[4,4096]{1,0:T(4,128)S(1)} %reshape.111), channel_id=1, source_target_pairs={{0,1},{1,0},{2,3},{3,2},{4,5},{5,4},{6,7},{7,6},{8,9},{9,8},{10,11... | collective-permute-start | bytes 196616 | tf_op jit(solution)/shard_map/ppermute | solution.py:40
  111.1 6.5 %collective-permute-start.1 = (f32[4,4096]{1,0:T(4,128)S(1)}, f32[4,4096]{1,0:T(4,128)S(1)}, u32[]{:S(2)}, u32[]{:S(2)}) collective-permute-start(f32[4,4096]{1,0:T(4,128)S(1)} %add.51), channel_id=1, source_target_pairs={{0,2},{1,3},{2,0},{3,1},{4,6},{5,7},{6,4},{7,5},{8,10},{9,11},{10,... | collective-permute-start | bytes 196616 | tf_op jit(solution)/shard_map/ppermute | solution.py:40
  117.6 8.9 %collective-permute-start.2 = (f32[4,4096]{1,0:T(4,128)S(1)}, f32[4,4096]{1,0:T(4,128)S(1)}, u32[]{:S(2)}, u32[]{:S(2)}) collective-permute-start(f32[4,4096]{1,0:T(4,128)S(1)} %add.52), channel_id=1, source_target_pairs={{0,4},{1,5},{2,6},{3,7},{4,0},{5,1},{6,2},{7,3},{8,12},{9,13},{10,... | collective-permute-start | bytes 196616 | tf_op jit(solution)/shard_map/ppermute | solution.py:40
  126.5 5.0 %collective-permute-start.3 = (f32[4,4096]{1,0:T(4,128)S(1)}, f32[4,4096]{1,0:T(4,128)S(1)}, u32[]{:S(2)}, u32[]{:S(2)}) collective-permute-start(f32[4,4096]{1,0:T(4,128)S(1)} %add.53), channel_id=1, source_target_pairs={{0,8},{1,9},{2,10},{3,11},{4,12},{5,13},{6,14},{7,15},{8,0},{9,1},... | collective-permute-start | bytes 196616 | tf_op jit(solution)/shard_map/ppermute | solution.py:40
  131.6 6.5 %collective-permute-start.4 = (f32[4,4096]{1,0:T(4,128)S(1)}, f32[4,4096]{1,0:T(4,128)S(1)}, u32[]{:S(2)}, u32[]{:S(2)}) collective-permute-start(f32[4,4096]{1,0:T(4,128)S(1)} %add.54), channel_id=1, source_target_pairs={{0,16},{1,17},{2,18},{3,19},{4,20},{5,21},{6,22},{7,23},{8,24},{9,... | collective-permute-start | bytes 196616 | tf_op jit(solution)/shard_map/ppermute | solution.py:40
  138.8 66.8 %copy-start.1 = (bf16[32,4096]{1,0:T(8,128)(2,1)S(1)}, bf16[32,4096]{1,0:T(8,128)(2,1)}, u32[]{:S(2)}) copy-start(bf16[32,4096]{1,0:T(8,128)(2,1)} %param.15) | copy-start | bytes 786436
  191.0 15.5 %copy-start.2 = (s32[64]{0:T(128)S(1)}, s32[64]{0:T(128)}, u32[]{:S(2)}) copy-start(s32[64]{0:T(128)} %param.12) | copy-start | bytes 772
Sparse Core Ops, SparseCore 0:
  10.5 84.9 all-gather.4
  138.9 50.5 all-gather.6
